TPU v7x, 32 devices: a whole 2x2x4 slice. The times are simulated.
32 devices in a mesh: dp: 4 (over z), section: 2 (over x), mp: 4 (over y, core).
Axes of the slice: x: 2, y: 2, z: 4, core: 2. Of those that a mesh axis runs over, the one named last changes fastest.
Arguments:
- source_rows: bfloat16 [1024, 1024], P('dp', 'mp'), may hold values from -6 to 6
- value_weight: bfloat16 [2, 1024, 1024], P('section', None, 'mp'), may hold values from -0.1875 to 0.1875
- gate_weight: bfloat16 [2, 1024, 1024], P('section', None, 'mp'), may hold values from -0.1875 to 0.1875
- kernel_weight: bfloat16 [2, 1024, 496], P('section', None, 'mp'), may hold values from -0.1875 to 0.1875
- segment_ids: int32 [8, 128], P('dp'), may hold values from 0 to 3, never falling along the last dimension, each value on 1 to 64 neighbouring positions
- out_grad: bfloat16 [1024, 1024], P('dp', 'mp'), may hold values from -6 to 6
Outputs:
- value_grad: float32 [2, 1024, 1024], P('section', 'dp', 'mp')
- gate_grad: float32 [2, 1024, 1024], P('section', 'dp', 'mp')
- kernel_grad: float32 [2, 1024, 496], P('section', 'dp', 'mp')
Inputs may be any that keep to these rules, and one draw needn't show every extreme that they name: `segment_ids`: in each microbatch row of 128 positions the sentence numbers never fall and every number from 0 up to the largest appears; a sentence covers 1 to 64 positions, and in every microbatch exactly one sentence covers 64 positions.
All inputs are finite; a program needn't handle non-finite values.
Results may differ from a plain program's by a relative error of at most 0.015.
Values may be sent and summed in bfloat16 or wider, within the bound.
A program may use at most 64 MiB of HBM per device.

v0:
```python
import jax
import jax.numpy as jnp
from jax import lax
from jax.sharding import PartitionSpec as P

KERNEL = 31


def from_behind(value, axis, steps):
    count = lax.axis_size(axis)
    initial, last = (max(0, -steps), min(count, count - steps))
    return lax.ppermute(value, axis, [(source, source + steps) for source in range(initial, last)])


def make_table(segments):
    row_count = segments.shape[0]
    positions = jnp.arange(row_count, dtype=jnp.int32)
    offsets = positions[None, :] - positions[:, None] + KERNEL // 2
    same_doc = segments[:, None] == segments[None, :]
    tap_index = jnp.arange(KERNEL, dtype=jnp.int32)[:, None, None]
    return ((offsets[None] == tap_index) & same_doc[None]).astype(jnp.float32)


def normalize(rows_in):
    widened = rows_in.astype(jnp.float32)
    row_mean = jnp.mean(widened, axis=-1, keepdims=True)
    centred = widened - row_mean
    inv_std = lax.rsqrt(jnp.mean(centred * centred, axis=-1, keepdims=True) + 1e-05)
    normed = centred * inv_std
    return (normed, inv_std, normed.astype(jnp.bfloat16))


def forward_pieces(normed_b, band_table, weights):
    w_value, w_gate, w_kernel = weights
    row_count = normed_b.shape[0]
    value_proj = jnp.dot(normed_b, w_value, preferred_element_type=jnp.float32)
    gate_proj = jnp.dot(normed_b, w_gate, preferred_element_type=jnp.float32)
    gate_sig = jax.nn.sigmoid(gate_proj)
    gated = (value_proj * gate_sig).astype(jnp.bfloat16)
    head_count = w_kernel.shape[1] // KERNEL
    head_size = w_value.shape[1] // head_count
    logits = jnp.dot(normed_b, w_kernel, preferred_element_type=jnp.float32).reshape(
        row_count, head_count, KERNEL
    )
    exp_logits = jnp.exp(logits)
    taps = exp_logits / jnp.sum(exp_logits, axis=-1, keepdims=True)
    band_mat = jnp.einsum(
        "thj,jts->hts",
        taps.astype(jnp.bfloat16),
        band_table.astype(jnp.bfloat16),
        preferred_element_type=jnp.float32,
    ).astype(jnp.bfloat16)
    gated3 = gated.reshape(row_count, head_count, head_size)
    mixed = jnp.einsum(
        "hts,shd->thd", band_mat, gated3, preferred_element_type=jnp.float32
    ).reshape(row_count, -1)
    return (value_proj, gate_sig, gated3, taps, band_mat, mixed)


def layer_forward(full_rows, segments, weights, mp_index):
    normed, inv_std, normed_b = normalize(full_rows)
    pieces = forward_pieces(normed_b, make_table(segments), weights)
    half_width = weights[0].shape[1]
    own_part = lax.dynamic_slice_in_dim(
        full_rows.astype(jnp.float32), mp_index * half_width, half_width, 1
    )
    return (own_part + pieces[5]).astype(jnp.bfloat16)


def layer_backward(normed_b, segments, grad_out, weights):
    w_value, w_gate, w_kernel = weights
    band_table = make_table(segments)
    value_proj, gate_sig, gated3, taps, band_mat, mixed = forward_pieces(
        normed_b, band_table, weights
    )
    row_count, head_count, head_size = gated3.shape
    grad_mixed = grad_out.astype(jnp.bfloat16).reshape(row_count, head_count, head_size)
    grad_gated = jnp.einsum(
        "hts,thd->shd", band_mat, grad_mixed, preferred_element_type=jnp.float32
    ).reshape(row_count, -1)
    tap_outer = jnp.einsum("thd,shd->hts", grad_mixed, gated3, preferred_element_type=jnp.float32)
    grad_taps = jnp.einsum("hts,jts->thj", tap_outer, band_table)
    grad_logits = (
        (taps * (grad_taps - jnp.sum(taps * grad_taps, axis=-1, keepdims=True)))
        .astype(jnp.bfloat16)
        .reshape(row_count, -1)
    )
    grad_value = (grad_gated * gate_sig).astype(jnp.bfloat16)
    grad_gate = (grad_gated * value_proj * gate_sig * (1.0 - gate_sig)).astype(jnp.bfloat16)
    dims = (((1,), (1,)), ((), ()))
    grad_part = lax.dot_general(grad_value, w_value, dims, preferred_element_type=jnp.float32)
    grad_part = grad_part + lax.dot_general(
        grad_gate, w_gate, dims, preferred_element_type=jnp.float32
    )
    grad_part = grad_part + lax.dot_general(
        grad_logits, w_kernel, dims, preferred_element_type=jnp.float32
    )
    return (grad_part, jnp.concatenate([grad_value, grad_gate, grad_logits], axis=1))


def shards(source_rows, value_weight, gate_weight, kernel_weight, segment_ids, out_grad):
    section_count = lax.axis_size("section")
    section_index = lax.axis_index("section")
    mp_index = lax.axis_index("mp")
    micro_count, row_count = segment_ids.shape
    full_width = value_weight.shape[1]
    half_width = value_weight.shape[2]
    weights = (value_weight[0], gate_weight[0], kernel_weight[0])
    term_width = 2 * half_width + kernel_weight.shape[2]
    inputs = source_rows.reshape(micro_count, row_count, half_width)
    top_grads = out_grad.reshape(micro_count, row_count, half_width)
    tick_count = micro_count + section_count - 1

    def forward_tick(tick, carry):
        received, stored = carry
        micro_index = tick - section_index
        active = (micro_index >= 0) & (micro_index < micro_count)
        slot_index = jnp.clip(micro_index, 0, micro_count - 1)
        own_rows = jnp.where(section_index == 0, inputs[slot_index], received)
        full_rows = lax.all_gather(own_rows, "mp", axis=1, tiled=True)
        segments = segment_ids[slot_index]
        result = lax.cond(
            active,
            lambda: layer_forward(full_rows, segments, weights, mp_index),
            lambda: jnp.zeros_like(own_rows),
        )
        stored = stored.at[slot_index].set(jnp.where(active, full_rows, stored[slot_index]))
        passed = from_behind(result, "section", 1)
        return (passed, stored)

    start_rows = jnp.zeros((row_count, half_width), jnp.bfloat16)
    start_store = jnp.zeros((micro_count, row_count, full_width), jnp.bfloat16)
    unused, stored = lax.fori_loop(0, tick_count, forward_tick, (start_rows, start_store))

    def backward_tick(tick, carry):
        received, grads, terms_store = carry
        micro_index = tick - (section_count - 1 - section_index)
        active = (micro_index >= 0) & (micro_index < micro_count)
        slot_index = jnp.clip(micro_index, 0, micro_count - 1)
        top_grad = top_grads[slot_index].astype(jnp.float32)
        grad_out = jnp.where(section_index == section_count - 1, top_grad, received)
        segments = segment_ids[slot_index]
        normed, inv_std, normed_b = normalize(stored[slot_index])
        grad_part, grad_terms = lax.cond(
            active,
            lambda: layer_backward(normed_b, segments, grad_out, weights),
            lambda: (
                jnp.zeros((row_count, full_width), jnp.float32),
                jnp.zeros((row_count, term_width), jnp.bfloat16),
            ),
        )
        grad_normed = lax.psum(grad_part.astype(jnp.bfloat16), "mp").astype(jnp.float32)
        norm_back = inv_std * (
            grad_normed
            - jnp.mean(grad_normed, axis=-1, keepdims=True)
            - normed * jnp.mean(grad_normed * normed, axis=-1, keepdims=True)
        )
        own_back = lax.dynamic_slice_in_dim(norm_back, mp_index * half_width, half_width, 1)
        grad_in = grad_out + own_back
        grad_in = jnp.where(active, grad_in, 0.0)
        grads = lax.cond(
            active,
            lambda: grads
            + lax.dot_general(
                normed_b, grad_terms, (((0,), (0,)), ((), ())), preferred_element_type=jnp.float32
            ),
            lambda: grads,
        )
        passed = from_behind(grad_in.astype(jnp.bfloat16), "section", -1).astype(grad_in.dtype)
        return (passed, grads, terms_store)

    start_grads = jnp.zeros((full_width, term_width), jnp.float32)
    start_terms = jnp.zeros((1,), jnp.bfloat16)
    start_back = jnp.zeros((row_count, half_width), jnp.float32)
    unused, grads, terms_store = lax.fori_loop(
        0, tick_count, backward_tick, (start_back, start_grads, start_terms)
    )
    shares = lax.psum_scatter(
        grads.astype(jnp.bfloat16), "dp", scatter_dimension=0, tiled=True
    ).astype(jnp.float32)
    value_share = shares[:, :half_width][None]
    gate_share = shares[:, half_width : 2 * half_width][None]
    kernel_share = shares[:, 2 * half_width :][None]
    return (value_share, gate_share, kernel_share)


def solution(mesh):
    in_specs = (
        P("dp", "mp"),
        P("section", None, "mp"),
        P("section", None, "mp"),
        P("section", None, "mp"),
        P("dp", None),
        P("dp", "mp"),
    )
    out_specs = (P("section", "dp", "mp"), P("section", "dp", "mp"), P("section", "dp", "mp"))
    return jax.shard_map(shards, mesh=mesh, in_specs=in_specs, out_specs=out_specs, check_vma=False)
```

profile of v0, /device:TPU:0, one launch (start us, length us, event | category | flops | bytes accessed | tf_op | source)
XLA Modules:
  0.0 359.8 jit_solution(7524102810339772016)
XLA Ops:
  8.1 50.1 %while.38 = (s32[]{:T(128)}, bf16[128,256]{0,1:T(8,128)(2,1)S(1)}, bf16[2,128,1024]{1,2,0:T(8,128)(2,1)S(1)}, s32[]{:T(128)}, pred[]{:T(512)}, /*index=5*/bf16[2...) while((s32[]{:T(128)}, bf16[128,256]{0,1:T(8,128)(2,1)S(1)}, ...), condition=%wide.region_7.8_spmd, body=%wide.region_0.7_spmd.sunk | while | flops 184383632 | bytes 11819549 | solution.py:133
  9.1 7.2 %all_gather.9 = bf16[128,1024]{0,1:T(8,128)(2,1)S(1)} all-gather(bf16[128,256]{0,1:T(8,128)(2,1)S(1)} %bitcast_select_fusion.4), channel_id=1, replica_groups=mesh['dp'=4,'section'=2,'mp'=4] {'mp'}, dimensions={1}, use_global_device_ids=true | all-gather | bytes 327680 | tf_op jit(solution)/shard_map/while/body/eval_jaxpr/all_gather | solution.py:120
  16.4 4.1 %conditional.8 = (bf16[128,256]{0,1:T(8,128)(2,1)S(1)}) conditional(s32[]{:T(128)} %convert_element_type.241, () %tuple.133, (bf16[128,1024]{0,1:T(8,128)(2,1)S(1)}, s32[]{:T(128)}, bf16[1024,256]{1,0:T(8,128)(2,1)}, bf16[1024,256]{1,0:T(8,128)(2,1)}, s32[2,128]{1,0:T(2,128)}, /*index=5*/s32[]{:T(128)}, bf16[1024,124]{1,0:T(8,128)(2,1)}) %tuple.134), branch_computations={%region_1.1_spmd, %region_2.5_spmd} | conditional | flops 184088704 | bytes 9459834 | solution.py:122
  24.9 5.8 %all_gather.9 = bf16[128,1024]{0,1:T(8,128)(2,1)S(1)} all-gather(bf16[128,256]{0,1:T(8,128)(2,1)S(1)} %bitcast_select_fusion.4), channel_id=1, replica_groups=mesh['dp'=4,'section'=2,'mp'=4] {'mp'}, dimensions={1}, use_global_device_ids=true | all-gather | bytes 327680 | tf_op jit(solution)/shard_map/while/body/eval_jaxpr/all_gather | solution.py:120
  30.7 4.1 %conditional.8 = (bf16[128,256]{0,1:T(8,128)(2,1)S(1)}) conditional(s32[]{:T(128)} %convert_element_type.241, () %tuple.133, (bf16[128,1024]{0,1:T(8,128)(2,1)S(1)}, s32[]{:T(128)}, bf16[1024,256]{1,0:T(8,128)(2,1)}, bf16[1024,256]{1,0:T(8,128)(2,1)}, s32[2,128]{1,0:T(2,128)}, /*index=5*/s32[]{:T(128)}, bf16[1024,124]{1,0:T(8,128)(2,1)}) %tuple.134), branch_computations={%region_1.1_spmd, %region_2.5_spmd} | conditional | flops 184088704 | bytes 9459834 | solution.py:122
  34.8 4.4 %collective-permute-start = (bf16[128,256]{0,1:T(8,128)(2,1)S(1)}, bf16[128,256]{0,1:T(8,128)(2,1)S(1)}, u32[]{:S(2)}, u32[]{:S(2)}) collective-permute-start(bf16[128,256]{0,1:T(8,128)(2,1)S(1)} %get-tuple-element.1041), channel_id=1, source_target_pairs={{0,4},{1,5},{2,6},{3,7},{8,12},{9,13},{10,14},{11,15},{16,20},{17,... | collective-permute-start | bytes 196616 | tf_op jit(solution)/shard_map/while/body/eval_jaxpr/ppermute | solution.py:12
  42.1 5.8 %all_gather.9 = bf16[128,1024]{0,1:T(8,128)(2,1)S(1)} all-gather(bf16[128,256]{0,1:T(8,128)(2,1)S(1)} %bitcast_select_fusion.4), channel_id=1, replica_groups=mesh['dp'=4,'section'=2,'mp'=4] {'mp'}, dimensions={1}, use_global_device_ids=true | all-gather | bytes 327680 | tf_op jit(solution)/shard_map/while/body/eval_jaxpr/all_gather | solution.py:120
  47.9 8.5 %collective-permute-start = (bf16[128,256]{0,1:T(8,128)(2,1)S(1)}, bf16[128,256]{0,1:T(8,128)(2,1)S(1)}, u32[]{:S(2)}, u32[]{:S(2)}) collective-permute-start(bf16[128,256]{0,1:T(8,128)(2,1)S(1)} %get-tuple-element.1041), channel_id=1, source_target_pairs={{0,4},{1,5},{2,6},{3,7},{8,12},{9,13},{10,14},{11,15},{16,20},{17,... | collective-permute-start | bytes 196616 | tf_op jit(solution)/shard_map/while/body/eval_jaxpr/ppermute | solution.py:12
  59.5 257.4 %while.39 = (s32[]{:T(128)}, f32[128,256]{1,0:T(8,128)}, f32[1024,636]{1,0:T(8,128)S(1)}, s32[]{:T(128)}, pred[]{:T(512)}, /*index=5*/bf16[2,128,256]{2,1,0:T(8,...) while((s32[]{:T(128)}, f32[128,256]{1,0:T(8,128)}, ...), condition=%wide.region_20.21_spmd.clone, body=%wide.region_8.20_spmd.clone.sunk | while | flops 533156512 | bytes 23325744 | solution.py:175
  65.9 71.7 %all-reduce.2.cloned.1.call-done = bf16[128,1024]{1,0:T(8,128)(2,1)} async-done(((bf16[128,1024]{1,0:T(8,128)(2,1)}), bf16[128,1024]{1,0:T(8,128)(2,1)}) %all-reduce.2.cloned.1.call-update) | async-done | bytes 262160 | tf_op jit(solution)/shard_map/while/body/eval_jaxpr/psum | solution.py:152
  141.8 4.8 %collective-permute-done.1 = bf16[128,256]{1,0:T(8,128)(2,1)S(1)} collective-permute-done((bf16[128,256]{1,0:T(8,128)(2,1)S(1)}, bf16[128,256]{1,0:T(8,128)(2,1)S(1)}, u32[]{:S(2)}, u32[]{:S(2)}) %collective-permute-start.1) | collective-permute-done | bytes 65568 | tf_op jit(solution)/shard_map/while/body/eval_jaxpr/ppermute | solution.py:12
  152.3 38.8 %conditional.9 = (bf16[128,1024]{1,0:T(8,128)(2,1)}, bf16[128,636]{1,0:T(8,128)(2,1)}) conditional(s32[]{:T(128)} %convert_element_type.248, () %tuple.138, (s32[2,128]{1,0:T(2,128)}, s32[]{:T(128)}, bf16[128,1024]{1,0:T(8,128)(2,1)}, bf16[1024,124]{1,0:T(8,128)(2,1)}, f32[128,256]{1,0:T(8,128)S(1)}, /*index=5*/bf16[1024,256]{1,0:T(8,128)(2,1)}, ...), branch_computations={%region_11.11_spmd, %region_12.14_spmd} | conditional | flops 362930720 | bytes 10925676 | solution.py:144
  160.7 2.0 fusion.23
  168.4 2.0 multiply_convert_fusion.4
  176.9 7.4 %fusion.20 = bf16[128,4,31]{2,1,0:T(4,128)(2,1)} fusion(f32[128,4,31]{2,1,0:T(4,128)S(1)} %fusion.16, f32[128,4,31]{2,1,0:T(4,128)} %copy.31, f32[128,4]{1,0:T(8,128)} %copy.30), kind=kOutput, calls=%fused_computation.45 | output fusion | flops 95774 | bytes 160768 | tf_op jit(solution)/shard_map/while/body/eval_jaxpr/cond/branch_1_fun/sub | solution.py:84
  191.1 31.2 %all-reduce.2.cloned.1.call-done = bf16[128,1024]{1,0:T(8,128)(2,1)} async-done(((bf16[128,1024]{1,0:T(8,128)(2,1)}), bf16[128,1024]{1,0:T(8,128)(2,1)}) %all-reduce.2.cloned.1.call-update) | async-done | bytes 262160 | tf_op jit(solution)/shard_map/while/body/eval_jaxpr/psum | solution.py:152
  228.3 3.1 collective-permute-done.1
  237.1 38.8 %conditional.9 = (bf16[128,1024]{1,0:T(8,128)(2,1)}, bf16[128,636]{1,0:T(8,128)(2,1)}) conditional(s32[]{:T(128)} %convert_element_type.248, () %tuple.138, (s32[2,128]{1,0:T(2,128)}, s32[]{:T(128)}, bf16[128,1024]{1,0:T(8,128)(2,1)}, bf16[1024,124]{1,0:T(8,128)(2,1)}, f32[128,256]{1,0:T(8,128)S(1)}, /*index=5*/bf16[1024,256]{1,0:T(8,128)(2,1)}, ...), branch_computations={%region_11.11_spmd, %region_12.14_spmd} | conditional | flops 362930720 | bytes 10925676 | solution.py:144
  245.5 2.0 fusion.23
  253.2 2.0 multiply_convert_fusion.4
  261.7 7.4 %fusion.20 = bf16[128,4,31]{2,1,0:T(4,128)(2,1)} fusion(f32[128,4,31]{2,1,0:T(4,128)S(1)} %fusion.16, f32[128,4,31]{2,1,0:T(4,128)} %copy.31, f32[128,4]{1,0:T(8,128)} %copy.30), kind=kOutput, calls=%fused_computation.45 | output fusion | flops 95774 | bytes 160768 | tf_op jit(solution)/shard_map/while/body/eval_jaxpr/cond/branch_1_fun/sub | solution.py:84
  275.9 31.2 %all-reduce.2.cloned.1.call-done = bf16[128,1024]{1,0:T(8,128)(2,1)} async-done(((bf16[128,1024]{1,0:T(8,128)(2,1)}), bf16[128,1024]{1,0:T(8,128)(2,1)}) %all-reduce.2.cloned.1.call-update) | async-done | bytes 262160 | tf_op jit(solution)/shard_map/while/body/eval_jaxpr/psum | solution.py:152
  313.1 3.1 collective-permute-done.1
  318.2 31.9 %reduce-scatter.2.cloned.1.call-done = bf16[256,636]{1,0:T(8,128)(2,1)} async-done(((bf16[1024,636]{1,0:T(8,128)(2,1)}), bf16[256,636]{1,0:T(8,128)(2,1)}) %reduce-scatter.2.cloned.1.call-update) | async-done | bytes 325648 | tf_op jit(solution)/shard_map/reduce_scatter | solution.py:178
  (213 shorter events, 117.2 us)
Async XLA Ops:
  16.4 5.5 %copy-start.9 = (s32[3]{0:T(128)S(1)}, s32[3]{0:T(128)}, u32[]{:S(2)}) copy-start(s32[3]{0:T(128)} %get-tuple-element.994) | copy-start | bytes 40 | tf_op jit(solution)/shard_map/while
  16.4 3.2 copy-start
  16.4 3.4 copy-start.5
  20.5 3.4 collective-permute-start
  30.7 8.6 %copy-start.9 = (s32[3]{0:T(128)S(1)}, s32[3]{0:T(128)}, u32[]{:S(2)}) copy-start(s32[3]{0:T(128)} %get-tuple-element.994) | copy-start | bytes 40 | tf_op jit(solution)/shard_map/while
  30.7 3.2 copy-start
  30.7 3.4 copy-start.5
  34.8 6.3 %collective-permute-start = (bf16[128,256]{0,1:T(8,128)(2,1)S(1)}, bf16[128,256]{0,1:T(8,128)(2,1)S(1)}, u32[]{:S(2)}, u32[]{:S(2)}) collective-permute-start(bf16[128,256]{0,1:T(8,128)(2,1)S(1)} %get-tuple-element.1041), channel_id=1, source_target_pairs={{0,4},{1,5},{2,6},{3,7},{8,12},{9,13},{10,14},{11,15},{16,20},{17,... | collective-permute-start | bytes 196616 | tf_op jit(solution)/shard_map/while/body/eval_jaxpr/ppermute | solution.py:12
  47.9 8.5 %copy-start.9 = (s32[3]{0:T(128)S(1)}, s32[3]{0:T(128)}, u32[]{:S(2)}) copy-start(s32[3]{0:T(128)} %get-tuple-element.994) | copy-start | bytes 40 | tf_op jit(solution)/shard_map/while
  47.9 10.4 %collective-permute-start = (bf16[128,256]{0,1:T(8,128)(2,1)S(1)}, bf16[128,256]{0,1:T(8,128)(2,1)S(1)}, u32[]{:S(2)}, u32[]{:S(2)}) collective-permute-start(bf16[128,256]{0,1:T(8,128)(2,1)S(1)} %get-tuple-element.1041), channel_id=1, source_target_pairs={{0,4},{1,5},{2,6},{3,7},{8,12},{9,13},{10,14},{11,15},{16,20},{17,... | collective-permute-start | bytes 196616 | tf_op jit(solution)/shard_map/while/body/eval_jaxpr/ppermute | solution.py:12
  58.3 1.2 copy-start.1
  59.5 78.1 %all-reduce.2.cloned.1.call-start = ((), (), s32[]{:S(2)}) async-start(), calls=%async_computation.2 | async-start | bytes 524288 | tf_op jit(solution)/shard_map/while/body/eval_jaxpr/psum | solution.py:152
  140.5 6.2 %collective-permute-start.1 = (bf16[128,256]{1,0:T(8,128)(2,1)S(1)}, bf16[128,256]{1,0:T(8,128)(2,1)S(1)}, u32[]{:S(2)}, u32[]{:S(2)}) collective-permute-start(bf16[128,256]{1,0:T(8,128)(2,1)S(1)} %fusion.74), channel_id=1, source_target_pairs={{4,0},{5,1},{6,2},{7,3},{12,8},{13,9},{14,10},{15,11},{20,16},{21,... | collective-permute-start | bytes 196616 | tf_op jit(solution)/shard_map/while/body/eval_jaxpr/ppermute | solution.py:12
  147.3 75.0 %all-reduce.2.cloned.1.call-start = ((), (), s32[]{:S(2)}) async-start(), calls=%async_computation.2 | async-start | bytes 524288 | tf_op jit(solution)/shard_map/while/body/eval_jaxpr/psum | solution.py:152
  164.4 1.5 copy-start.4
  186.0 4.2 %copy-start.2 = (bf16[1024,124]{1,0:T(8,128)(2,1)S(1)}, bf16[1024,124]{1,0:T(8,128)(2,1)}, u32[]{:S(2)}) copy-start(bf16[1024,124]{1,0:T(8,128)(2,1)} %get-tuple-element.579) | copy-start | bytes 761860 | tf_op jit(solution)/shard_map/while/body/eval_jaxpr/cond
  186.0 4.2 %copy-start.6 = (bf16[128,124]{1,0:T(8,128)(2,1)S(1)}, bf16[128,124]{1,0:T(8,128)(2,1)}, u32[]{:S(2)}) copy-start(bf16[128,124]{1,0:T(8,128)(2,1)} %reshape.248) | copy-start | bytes 95236 | tf_op jit(solution)/shard_map/while/body/eval_jaxpr/cond
  225.3 6.2 %collective-permute-start.1 = (bf16[128,256]{1,0:T(8,128)(2,1)S(1)}, bf16[128,256]{1,0:T(8,128)(2,1)S(1)}, u32[]{:S(2)}, u32[]{:S(2)}) collective-permute-start(bf16[128,256]{1,0:T(8,128)(2,1)S(1)} %fusion.74), channel_id=1, source_target_pairs={{4,0},{5,1},{6,2},{7,3},{12,8},{13,9},{14,10},{15,11},{20,16},{21,... | collective-permute-start | bytes 196616 | tf_op jit(solution)/shard_map/while/body/eval_jaxpr/ppermute | solution.py:12
  232.1 75.0 %all-reduce.2.cloned.1.call-start = ((), (), s32[]{:S(2)}) async-start(), calls=%async_computation.2 | async-start | bytes 524288 | tf_op jit(solution)/shard_map/while/body/eval_jaxpr/psum | solution.py:152
  249.2 1.5 copy-start.4
  270.8 4.2 %copy-start.2 = (bf16[1024,124]{1,0:T(8,128)(2,1)S(1)}, bf16[1024,124]{1,0:T(8,128)(2,1)}, u32[]{:S(2)}) copy-start(bf16[1024,124]{1,0:T(8,128)(2,1)} %get-tuple-element.579) | copy-start | bytes 761860 | tf_op jit(solution)/shard_map/while/body/eval_jaxpr/cond
  270.8 4.2 %copy-start.6 = (bf16[128,124]{1,0:T(8,128)(2,1)S(1)}, bf16[128,124]{1,0:T(8,128)(2,1)}, u32[]{:S(2)}) copy-start(bf16[128,124]{1,0:T(8,128)(2,1)} %reshape.248) | copy-start | bytes 95236 | tf_op jit(solution)/shard_map/while/body/eval_jaxpr/cond
  310.1 6.2 %collective-permute-start.1 = (bf16[128,256]{1,0:T(8,128)(2,1)S(1)}, bf16[128,256]{1,0:T(8,128)(2,1)S(1)}, u32[]{:S(2)}, u32[]{:S(2)}) collective-permute-start(bf16[128,256]{1,0:T(8,128)(2,1)S(1)} %fusion.74), channel_id=1, source_target_pairs={{4,0},{5,1},{6,2},{7,3},{12,8},{13,9},{14,10},{15,11},{20,16},{21,... | collective-permute-start | bytes 196616 | tf_op jit(solution)/shard_map/while/body/eval_jaxpr/ppermute | solution.py:12
  316.9 33.1 %reduce-scatter.2.cloned.1.call-start = ((), (), s32[]{:S(2)}) async-start(), calls=%async_computation.1 | async-start | bytes 1638400 | tf_op jit(solution)/shard_map/reduce_scatter | solution.py:178
  (7 other events, 7.0 us)
Sparse Core Ops, SparseCore 0:
  66.0 71.5 all-reduce.1
  191.3 31.0 all-reduce.1
  276.0 31.0 all-reduce.1
Sparse Core Ops, SparseCore 1:
  319.7 30.3 reduce-scatter.1
where the time goes:
time: 362 us; the launch traced here: 360 us
  waiting for transfers between devices  179 us (49%)
  other arithmetic  47.1 us (13%)
  local copies, waits for them, and re-layouts  42.7 us (12%)
  matrix products  38.4 us (11%)
  blocking collectives  18.8 us (5%)
  starting transfers between devices  18 us (5%)
  between operations  15.2 us (4%)
    psum x3, waiting for transfers between devices, backward_tick(): lax.psum(grad_part.astype(jnp.bfloat16), 'mp').astype(jnp.float32)  134 us
    reduce_scatter x1, waiting for transfers between devices, shards(): lax.psum_scatter(grads.astype(jnp.bfloat16), 'dp', scatter_dimension=0, t...  31.9 us
    all_gather x3, blocking collectives, forward_tick(): full_rows = lax.all_gather(own_rows, 'mp', axis=1, tiled=True)  18.8 us
    ppermute x6, starting transfers between devices, from_behind(): lax.ppermute(value, axis, [(source, source + steps) for source in range(i...  18 us
    sub x2, other arithmetic, layer_backward(): grad_taps - jnp.sum(taps * grad_taps, axis=-1, keepdims=True)  14.8 us
    ppermute x6, waiting for transfers between devices, from_behind(): lax.ppermute(value, axis, [(source, source + steps) for source in range(i...  12.7 us
    dynamic_slice x6, local copies, waits for them, and re-layouts, backward_tick(): normed, inv_std, normed_b = normalize(stored[slot_index])  8.26 us
  transfers between devices with their start and end apart: 10, of which 10 were waited for; matrix products, arithmetic and copies ran while one was open for 2% of the time, Pallas kernels for 0%

commit v1 on v0

--- a/solution.py
+++ b/solution.py
@@ -4,6 +4,28 @@
 from jax.sharding import PartitionSpec as P
 
 KERNEL = 31
+
+
+def in_order(blocks, dim):
+    blocks = jnp.moveaxis(blocks, 0, dim)
+    lengths = blocks.shape
+    return blocks.reshape(*lengths[:dim], lengths[dim] * lengths[dim + 1], *lengths[dim + 2 :])
+
+
+def grow_blocks(x, axis):
+    size = lax.axis_size(axis)
+    blocks = x[None]
+    for level in range(size.bit_length() - 1):
+        stride = 1 << level
+        partner_block = lax.ppermute(blocks, axis, [(i, i ^ stride) for i in range(size)])
+        both = jnp.stack([blocks, partner_block])
+        upper = lax.axis_index(axis) >> level & 1
+        blocks = jnp.where(upper == 0, both, both[::-1]).reshape(-1, *x.shape)
+    return blocks
+
+
+def doubled_up(x, axis, dim):
+    return in_order(grow_blocks(x, axis), dim)
 
 
 def from_behind(value, axis, steps):
@@ -117,7 +139,7 @@
         active = (micro_index >= 0) & (micro_index < micro_count)
         slot_index = jnp.clip(micro_index, 0, micro_count - 1)
         own_rows = jnp.where(section_index == 0, inputs[slot_index], received)
-        full_rows = lax.all_gather(own_rows, "mp", axis=1, tiled=True)
+        full_rows = doubled_up(own_rows, "mp", 1)
         segments = segment_ids[slot_index]
         result = lax.cond(
             active,

time: 362 us -> 373 us (1.030)
  blocking collectives: 18.8 us -> 0 us
  other arithmetic: 47.1 us -> 64.2 us
  waiting for transfers between devices: 179 us -> 192 us
  starting transfers between devices: 18 us -> 26.6 us
  local copies, waits for them, and re-layouts: 42.7 us -> 36.2 us
    all_gather x3 -> x0, blocking collectives: 18.8 us -> none  [forward_tick(): full_rows = lax.all_gather(own_rows, 'mp', axis=1, tiled=True)]
    ppermute x0 -> x6, waiting for transfers between devices: none -> 10.6 us  [grow_blocks(): lax.ppermute(blocks, axis, [(i, i ^ stride) for i in range(size)])]
    dynamic_slice x9 -> x0, local copies, waits for them, and re-layouts: 8.34 us -> none  [the longest x6 8.26 us: backward_tick(): normed, inv_std, normed_b = normalize(stored[slot_index])]
    ppermute x0 -> x6, starting transfers between devices: none -> 7.2 us  [grow_blocks(): lax.ppermute(blocks, axis, [(i, i ^ stride) for i in range(size)])]
    reduce_sum x5, other arithmetic: 0.96 us -> 7.26 us  [normalize(): jnp.mean(centred * centred, axis=-1, keepdims=True) + 1e-05]
    reduce_sum x5, other arithmetic: 0.65 us -> 5.26 us  [normalize(): row_mean = jnp.mean(widened, axis=-1, keepdims=True)]
  transfers between devices with their start and end apart: 10 -> 16, of which waited for: 10 -> 16; matrix products, arithmetic and copies ran while one was open for 2% -> 3% of each run, Pallas kernels for 0% -> 0%
where the time goes in v1:
time: 373 us; the launch traced here: 371 us
  waiting for transfers between devices  192 us (51%)
  other arithmetic  64.2 us (17%)
  local copies, waits for them, and re-layouts  36.2 us (10%)
  matrix products  35.8 us (10%)
  starting transfers between devices  26.6 us (7%)
  between operations  15.2 us (4%)
    psum x3, waiting for transfers between devices, backward_tick(): lax.psum(grad_part.astype(jnp.bfloat16), 'mp').astype(jnp.float32)  134 us
    reduce_scatter x1, waiting for transfers between devices, shards(): lax.psum_scatter(grads.astype(jnp.bfloat16), 'dp', scatter_dimension=0, t...  31.9 us
    ppermute x6, starting transfers between devices, from_behind(): lax.ppermute(value, axis, [(source, source + steps) for source in range(i...  19.4 us
    ppermute x6, waiting for transfers between devices, from_behind(): lax.ppermute(value, axis, [(source, source + steps) for source in range(i...  15.3 us
    sub x2, other arithmetic, layer_backward(): grad_taps - jnp.sum(taps * grad_taps, axis=-1, keepdims=True)  14.7 us
    ppermute x6, waiting for transfers between devices, grow_blocks(): lax.ppermute(blocks, axis, [(i, i ^ stride) for i in range(size)])  10.6 us
  transfers between devices with their start and end apart: 16, of which 16 were waited for; matrix products, arithmetic and copies ran while one was open for 3% of the time, Pallas kernels for 0%

profile of v1, /device:TPU:0, one launch (start us, length us, event | category | flops | bytes accessed | tf_op | source)
XLA Modules:
  0.0 370.9 jit_solution(9619249611985128554)
XLA Ops:
  9.2 59.7 %while.38 = (s32[]{:T(128)}, bf16[128,256]{0,1:T(8,128)(2,1)S(1)}, bf16[2,128,1024]{2,1,0:T(8,128)(2,1)S(1)}, s32[]{:T(128)}, pred[]{:T(512)}, /*index=5*/bf16[2...) while((s32[]{:T(128)}, bf16[128,256]{0,1:T(8,128)(2,1)S(1)}, ...), condition=%wide.region_7.8_spmd, body=%wide.region_0.7_spmd.sunk | while | flops 184383648 | bytes 16466581 | solution.py:155
  11.8 2.9 collective-permute-start.1
  16.2 2.4 collective-permute-done.1
  19.1 5.7 %conditional.8 = (bf16[128,256]{0,1:T(8,128)(2,1)S(1)}) conditional(s32[]{:T(128)} %convert_element_type.252, () %tuple.138, (bf16[128,4,256]{2,1,0:T(4,128)(2,1)S(1)}, s32[]{:T(128)}, bf16[1024,256]{1,0:T(8,128)(2,1)S(1)}, bf16[1024,256]{1,0:T(8,128)(2,1)S(1)}, s32[2,128]{1,0:T(2,128)S(1)}, /*index=5*/s32[]{:T(128)}, ...), branch_computations={%region_1.1_spmd, %region_2.5_spmd} | conditional | flops 183695488 | bytes 7155774 | solution.py:144
  33.7 2.4 collective-permute-done.1
  36.6 5.7 %conditional.8 = (bf16[128,256]{0,1:T(8,128)(2,1)S(1)}) conditional(s32[]{:T(128)} %convert_element_type.252, () %tuple.138, (bf16[128,4,256]{2,1,0:T(4,128)(2,1)S(1)}, s32[]{:T(128)}, bf16[1024,256]{1,0:T(8,128)(2,1)S(1)}, bf16[1024,256]{1,0:T(8,128)(2,1)S(1)}, s32[2,128]{1,0:T(2,128)S(1)}, /*index=5*/s32[]{:T(128)}, ...), branch_computations={%region_1.1_spmd, %region_2.5_spmd} | conditional | flops 183695488 | bytes 7155774 | solution.py:144
  42.3 4.3 %collective-permute-start.2 = (bf16[128,256]{0,1:T(8,128)(2,1)S(1)}, bf16[128,256]{0,1:T(8,128)(2,1)S(1)}, u32[]{:S(2)}, u32[]{:S(2)}) collective-permute-start(bf16[128,256]{0,1:T(8,128)(2,1)S(1)} %get-tuple-element.1034), channel_id=1, source_target_pairs={{0,4},{1,5},{2,6},{3,7},{8,12},{9,13},{10,14},{11,15},{16,20},{17,... | collective-permute-start | bytes 196616 | tf_op jit(solution)/shard_map/while/body/eval_jaxpr/ppermute | solution.py:34
  54.2 2.4 collective-permute-done.1
  57.1 10.0 %collective-permute-start.2 = (bf16[128,256]{0,1:T(8,128)(2,1)S(1)}, bf16[128,256]{0,1:T(8,128)(2,1)S(1)}, u32[]{:S(2)}, u32[]{:S(2)}) collective-permute-start(bf16[128,256]{0,1:T(8,128)(2,1)S(1)} %get-tuple-element.1034), channel_id=1, source_target_pairs={{0,4},{1,5},{2,6},{3,7},{8,12},{9,13},{10,14},{11,15},{16,20},{17,... | collective-permute-start | bytes 196616 | tf_op jit(solution)/shard_map/while/body/eval_jaxpr/ppermute | solution.py:34
  70.2 257.9 %while.39 = (s32[]{:T(128)}, f32[128,256]{1,0:T(8,128)}, f32[1024,636]{1,0:T(8,128)S(1)}, s32[]{:T(128)}, pred[]{:T(512)}, /*index=5*/bf16[2,128,256]{2,1,0:T(8,...) while((s32[]{:T(128)}, f32[128,256]{1,0:T(8,128)}, ...), condition=%wide.region_20.21_spmd.clone, body=%wide.region_8.20_spmd.clone.sunk | while | flops 533156512 | bytes 22277180 | solution.py:197
  76.0 71.5 %all-reduce.2.cloned.1.call-done = bf16[128,1024]{1,0:T(8,128)(2,1)} async-done(((bf16[128,1024]{1,0:T(8,128)(2,1)}), bf16[128,1024]{1,0:T(8,128)(2,1)}) %all-reduce.2.cloned.1.call-update) | async-done | bytes 262160 | tf_op jit(solution)/shard_map/while/body/eval_jaxpr/psum | solution.py:174
  152.5 5.0 %collective-permute-done.3 = bf16[128,256]{1,0:T(8,128)(2,1)S(1)} collective-permute-done((bf16[128,256]{1,0:T(8,128)(2,1)}, bf16[128,256]{1,0:T(8,128)(2,1)S(1)}, u32[]{:S(2)}, u32[]{:S(2)}) %collective-permute-start.3) | collective-permute-done | bytes 65568 | tf_op jit(solution)/shard_map/while/body/eval_jaxpr/ppermute | solution.py:34
  162.7 38.5 %conditional.9 = (bf16[128,1024]{1,0:T(8,128)(2,1)}, bf16[128,636]{1,0:T(8,128)(2,1)}) conditional(s32[]{:T(128)} %convert_element_type.259, () %tuple.143, (s32[2,128]{1,0:T(2,128)}, s32[]{:T(128)}, bf16[128,1024]{1,0:T(8,128)(2,1)S(1)}, bf16[1024,124]{1,0:T(8,128)(2,1)}, f32[128,256]{1,0:T(8,128)S(1)}, /*index=5*/bf16[1024,256]{1,0:T(8,128)(2,1)}, ...), branch_computations={%region_11.11_spmd, %region_12.14_spmd} | conditional | flops 362930720 | bytes 10925676 | solution.py:166
  171.0 1.9 fusion.27
  178.6 1.9 multiply_convert_fusion.4
  187.1 7.3 %fusion.24 = bf16[128,4,31]{2,1,0:T(4,128)(2,1)} fusion(f32[128,4,31]{2,1,0:T(4,128)S(1)} %fusion.20, f32[128,4,31]{2,1,0:T(4,128)} %copy.37, f32[128,4]{1,0:T(8,128)} %copy.36), kind=kOutput, calls=%fused_computation.52 | output fusion | flops 95774 | bytes 160768 | tf_op jit(solution)/shard_map/while/body/eval_jaxpr/cond/branch_1_fun/sub | solution.py:106
  201.2 31.2 %all-reduce.2.cloned.1.call-done = bf16[128,1024]{1,0:T(8,128)(2,1)} async-done(((bf16[128,1024]{1,0:T(8,128)(2,1)}), bf16[128,1024]{1,0:T(8,128)(2,1)}) %all-reduce.2.cloned.1.call-update) | async-done | bytes 262160 | tf_op jit(solution)/shard_map/while/body/eval_jaxpr/psum | solution.py:174
  239.1 3.4 collective-permute-done.3
  247.6 38.5 %conditional.9 = (bf16[128,1024]{1,0:T(8,128)(2,1)}, bf16[128,636]{1,0:T(8,128)(2,1)}) conditional(s32[]{:T(128)} %convert_element_type.259, () %tuple.143, (s32[2,128]{1,0:T(2,128)}, s32[]{:T(128)}, bf16[128,1024]{1,0:T(8,128)(2,1)S(1)}, bf16[1024,124]{1,0:T(8,128)(2,1)}, f32[128,256]{1,0:T(8,128)S(1)}, /*index=5*/bf16[1024,256]{1,0:T(8,128)(2,1)}, ...), branch_computations={%region_11.11_spmd, %region_12.14_spmd} | conditional | flops 362930720 | bytes 10925676 | solution.py:166
  255.9 1.9 fusion.27
  271.9 7.3 %fusion.24 = bf16[128,4,31]{2,1,0:T(4,128)(2,1)} fusion(f32[128,4,31]{2,1,0:T(4,128)S(1)} %fusion.20, f32[128,4,31]{2,1,0:T(4,128)} %copy.37, f32[128,4]{1,0:T(8,128)} %copy.36), kind=kOutput, calls=%fused_computation.52 | output fusion | flops 95774 | bytes 160768 | tf_op jit(solution)/shard_map/while/body/eval_jaxpr/cond/branch_1_fun/sub | solution.py:106
  286.1 31.2 %all-reduce.2.cloned.1.call-done = bf16[128,1024]{1,0:T(8,128)(2,1)} async-done(((bf16[128,1024]{1,0:T(8,128)(2,1)}), bf16[128,1024]{1,0:T(8,128)(2,1)}) %all-reduce.2.cloned.1.call-update) | async-done | bytes 262160 | tf_op jit(solution)/shard_map/while/body/eval_jaxpr/psum | solution.py:174
  324.0 3.4 collective-permute-done.3
  329.3 31.9 %reduce-scatter.2.cloned.1.call-done = bf16[256,636]{1,0:T(8,128)(2,1)} async-done(((bf16[1024,636]{1,0:T(8,128)(2,1)}), bf16[256,636]{1,0:T(8,128)(2,1)}) %reduce-scatter.2.cloned.1.call-update) | async-done | bytes 325648 | tf_op jit(solution)/shard_map/reduce_scatter | solution.py:200
  (238 shorter events, 136.8 us)
Async XLA Ops:
  9.2 9.8 %copy-start = (bf16[1024,256]{1,0:T(8,128)(2,1)S(1)}, bf16[1024,256]{1,0:T(8,128)(2,1)}, u32[]{:S(2)}) copy-start(bf16[1024,256]{1,0:T(8,128)(2,1)} %get-tuple-element.979) | copy-start | bytes 1572868 | tf_op jit(solution)/shard_map/while
  9.2 9.8 %copy-start.3 = (bf16[1024,256]{1,0:T(8,128)(2,1)S(1)}, bf16[1024,256]{1,0:T(8,128)(2,1)}, u32[]{:S(2)}) copy-start(bf16[1024,256]{1,0:T(8,128)(2,1)} %get-tuple-element.980) | copy-start | bytes 1572868 | tf_op jit(solution)/shard_map/while
  9.3 9.8 %copy-start.9 = (s32[2,128]{1,0:T(2,128)S(1)}, s32[2,128]{1,0:T(2,128)}, u32[]{:S(2)}) copy-start(s32[2,128]{1,0:T(2,128)} %get-tuple-element.981) | copy-start | bytes 3076 | tf_op jit(solution)/shard_map/while
  10.3 1.4 collective-permute-start
  11.8 6.8 %collective-permute-start.1 = (bf16[2,128,256]{1,2,0:T(8,128)(2,1)S(1)}, bf16[2,128,256]{1,2,0:T(8,128)(2,1)S(1)}, u32[]{:S(2)}, u32[]{:S(2)}) collective-permute-start(bf16[2,128,256]{1,2,0:T(8,128)(2,1)S(1)} %get-tuple-element.913), channel_id=1, source_target_pairs={{0,2},{1,3},{2,0},{3,1},{4,6},{5,7},{6,4},{7,5},{8,10},{9,11},{10,... | collective-permute-start | bytes 393224 | tf_op jit(solution)/shard_map/while/body/eval_jaxpr/ppermute | solution.py:20
  24.8 3.2 collective-permute-start.2
  28.0 8.6 %copy-start = (bf16[1024,256]{1,0:T(8,128)(2,1)S(1)}, bf16[1024,256]{1,0:T(8,128)(2,1)}, u32[]{:S(2)}) copy-start(bf16[1024,256]{1,0:T(8,128)(2,1)} %get-tuple-element.979) | copy-start | bytes 1572868 | tf_op jit(solution)/shard_map/while
  28.0 8.6 %copy-start.3 = (bf16[1024,256]{1,0:T(8,128)(2,1)S(1)}, bf16[1024,256]{1,0:T(8,128)(2,1)}, u32[]{:S(2)}) copy-start(bf16[1024,256]{1,0:T(8,128)(2,1)} %get-tuple-element.980) | copy-start | bytes 1572868 | tf_op jit(solution)/shard_map/while
  28.0 8.6 %copy-start.9 = (s32[2,128]{1,0:T(2,128)S(1)}, s32[2,128]{1,0:T(2,128)}, u32[]{:S(2)}) copy-start(s32[2,128]{1,0:T(2,128)} %get-tuple-element.981) | copy-start | bytes 3076 | tf_op jit(solution)/shard_map/while
  29.1 1.3 collective-permute-start
  30.5 5.6 %collective-permute-start.1 = (bf16[2,128,256]{1,2,0:T(8,128)(2,1)S(1)}, bf16[2,128,256]{1,2,0:T(8,128)(2,1)S(1)}, u32[]{:S(2)}, u32[]{:S(2)}) collective-permute-start(bf16[2,128,256]{1,2,0:T(8,128)(2,1)S(1)} %get-tuple-element.913), channel_id=1, source_target_pairs={{0,2},{1,3},{2,0},{3,1},{4,6},{5,7},{6,4},{7,5},{8,10},{9,11},{10,... | collective-permute-start | bytes 393224 | tf_op jit(solution)/shard_map/while/body/eval_jaxpr/ppermute | solution.py:20
  42.3 6.2 %collective-permute-start.2 = (bf16[128,256]{0,1:T(8,128)(2,1)S(1)}, bf16[128,256]{0,1:T(8,128)(2,1)S(1)}, u32[]{:S(2)}, u32[]{:S(2)}) collective-permute-start(bf16[128,256]{0,1:T(8,128)(2,1)S(1)} %get-tuple-element.1034), channel_id=1, source_target_pairs={{0,4},{1,5},{2,6},{3,7},{8,12},{9,13},{10,14},{11,15},{16,20},{17,... | collective-permute-start | bytes 196616 | tf_op jit(solution)/shard_map/while/body/eval_jaxpr/ppermute | solution.py:34
  48.5 8.6 %copy-start.3 = (bf16[1024,256]{1,0:T(8,128)(2,1)S(1)}, bf16[1024,256]{1,0:T(8,128)(2,1)}, u32[]{:S(2)}) copy-start(bf16[1024,256]{1,0:T(8,128)(2,1)} %get-tuple-element.980) | copy-start | bytes 1572868 | tf_op jit(solution)/shard_map/while
  48.5 8.6 %copy-start.9 = (s32[2,128]{1,0:T(2,128)S(1)}, s32[2,128]{1,0:T(2,128)}, u32[]{:S(2)}) copy-start(s32[2,128]{1,0:T(2,128)} %get-tuple-element.981) | copy-start | bytes 3076 | tf_op jit(solution)/shard_map/while
  49.6 1.3 collective-permute-start
  51.0 5.6 %collective-permute-start.1 = (bf16[2,128,256]{1,2,0:T(8,128)(2,1)S(1)}, bf16[2,128,256]{1,2,0:T(8,128)(2,1)S(1)}, u32[]{:S(2)}, u32[]{:S(2)}) collective-permute-start(bf16[2,128,256]{1,2,0:T(8,128)(2,1)S(1)} %get-tuple-element.913), channel_id=1, source_target_pairs={{0,2},{1,3},{2,0},{3,1},{4,6},{5,7},{6,4},{7,5},{8,10},{9,11},{10,... | collective-permute-start | bytes 393224 | tf_op jit(solution)/shard_map/while/body/eval_jaxpr/ppermute | solution.py:20
  57.1 11.8 %collective-permute-start.2 = (bf16[128,256]{0,1:T(8,128)(2,1)S(1)}, bf16[128,256]{0,1:T(8,128)(2,1)S(1)}, u32[]{:S(2)}, u32[]{:S(2)}) collective-permute-start(bf16[128,256]{0,1:T(8,128)(2,1)S(1)} %get-tuple-element.1034), channel_id=1, source_target_pairs={{0,4},{1,5},{2,6},{3,7},{8,12},{9,13},{10,14},{11,15},{16,20},{17,... | collective-permute-start | bytes 196616 | tf_op jit(solution)/shard_map/while/body/eval_jaxpr/ppermute | solution.py:34
  70.2 77.3 %all-reduce.2.cloned.1.call-start = ((), (), s32[]{:S(2)}) async-start(), calls=%async_computation.2 | async-start | bytes 524288 | tf_op jit(solution)/shard_map/while/body/eval_jaxpr/psum | solution.py:174
  151.2 6.4 %collective-permute-start.3 = (bf16[128,256]{1,0:T(8,128)(2,1)}, bf16[128,256]{1,0:T(8,128)(2,1)S(1)}, u32[]{:S(2)}, u32[]{:S(2)}) collective-permute-start(bf16[128,256]{1,0:T(8,128)(2,1)} %fusion.84), channel_id=1, source_target_pairs={{4,0},{5,1},{6,2},{7,3},{12,8},{13,9},{14,10},{15,11},{20,16},{21,... | collective-permute-start | bytes 196616 | tf_op jit(solution)/shard_map/while/body/eval_jaxpr/ppermute | solution.py:34
  158.3 74.1 %all-reduce.2.cloned.1.call-start = ((), (), s32[]{:S(2)}) async-start(), calls=%async_computation.2 | async-start | bytes 524288 | tf_op jit(solution)/shard_map/while/body/eval_jaxpr/psum | solution.py:174
  236.1 6.4 %collective-permute-start.3 = (bf16[128,256]{1,0:T(8,128)(2,1)}, bf16[128,256]{1,0:T(8,128)(2,1)S(1)}, u32[]{:S(2)}, u32[]{:S(2)}) collective-permute-start(bf16[128,256]{1,0:T(8,128)(2,1)} %fusion.84), channel_id=1, source_target_pairs={{4,0},{5,1},{6,2},{7,3},{12,8},{13,9},{14,10},{15,11},{20,16},{21,... | collective-permute-start | bytes 196616 | tf_op jit(solution)/shard_map/while/body/eval_jaxpr/ppermute | solution.py:34
  243.2 74.1 %all-reduce.2.cloned.1.call-start = ((), (), s32[]{:S(2)}) async-start(), calls=%async_computation.2 | async-start | bytes 524288 | tf_op jit(solution)/shard_map/while/body/eval_jaxpr/psum | solution.py:174
  321.0 6.4 %collective-permute-start.3 = (bf16[128,256]{1,0:T(8,128)(2,1)}, bf16[128,256]{1,0:T(8,128)(2,1)S(1)}, u32[]{:S(2)}, u32[]{:S(2)}) collective-permute-start(bf16[128,256]{1,0:T(8,128)(2,1)} %fusion.84), channel_id=1, source_target_pairs={{4,0},{5,1},{6,2},{7,3},{12,8},{13,9},{14,10},{15,11},{20,16},{21,... | collective-permute-start | bytes 196616 | tf_op jit(solution)/shard_map/while/body/eval_jaxpr/ppermute | solution.py:34
  328.1 33.1 %reduce-scatter.2.cloned.1.call-start = ((), (), s32[]{:S(2)}) async-start(), calls=%async_computation.1 | async-start | bytes 1638400 | tf_op jit(solution)/shard_map/reduce_scatter | solution.py:200
  (15 other events, 46.5 us)
Sparse Core Ops, SparseCore 0:
  76.1 71.3 all-reduce.1
  201.3 31.0 all-reduce.1
  286.2 31.0 all-reduce.1
Sparse Core Ops, SparseCore 1:
  330.8 30.3 reduce-scatter.1
